TPU v7x, 512 devices: a whole 4x8x8 slice. The times are simulated.
512 devices in a mesh: head: 8 (over z), blk: 64 (over x, y, core).
Axes of the slice: x: 4, y: 8, z: 8, core: 2. Of those that a mesh axis runs over, the one named last changes fastest.
Arguments:
- vision: bfloat16 [4, 1408, 8192], P(None, 'head', 'blk'), may hold values from -600 to 600
- ln_gain: float32 [1408], P('head'), may hold values from 0.5 to 1.5
- merge_proj: bfloat16 [4, 1408, 1408], P(None, 'head'), may hold values from -0.078125 to 0.078125
- image_slot: int32 [2048], P('blk'), may hold values from 0 to 32764, as said below
- text: bfloat16 [1408, 32768], P('head', 'blk'), may hold values from -600 to 600
- rms_gain: float32 [1408], replicated, may hold values from 0.5 to 1.5
- wqkv: bfloat16 [3, 1408, 1408], P(None, 'head'), may hold values from -0.31835938 to 0.31835938
- pcache: bfloat16 [2, 1408, 131072], P(None, 'head', 'blk'), may hold values from -300 to 300
- block_table: int32 [64, 128], replicated, may hold values from -1 to 4095, as said below
- cache_len: int32 [64], P('blk'), may hold values from 1 to 4096, as said below
Outputs:
- attended: bfloat16 [1408, 32768], P('head', 'blk')
- new_cache: bfloat16 [2, 1408, 32768], P(None, 'head', 'blk')
Inputs may be any that keep to these rules, and one draw needn't show every extreme that they name: `image_slot`: pieces never intersect and start at multiples of 4; the 32 pieces held by one index of blk start in the rows of 32 different requests, and every request receives exactly 32 pieces. `block_table`: row r holds a block number for j < ceil(cache_len[r] / 32) and -1 after; no block number appears twice; index d of blk holds blocks d * 64 to (d+1) * 64 - 1. The longest request has exactly 2 blocks on every index of blk; every other request has at most one block on any index. `cache_len`: exactly one request, the longest, has 4096 cached positions; all others have fewer.
All inputs are finite; a program needn't handle non-finite values.
Results may differ from a plain program's by a relative error of at most 0.025.
The roundings to bfloat16 on the way count: a program that leaves them out, or rounds other values in their place, can miss the bound.
Values may be sent and summed in bfloat16 or wider, within the bound.
A program may use at most 128 MiB of HBM per device.

v0:
```python
import math
import jax
import jax.numpy as jnp
from jax import lax
from jax.sharding import PartitionSpec as P

D = 1408
HD = 88
BS = 32
masked_score = -1e30


def rotary_columns(values, places):
    half = values.shape[1] // 2
    freq_index = jnp.arange(half, dtype=jnp.float32)
    inverse = jnp.exp(freq_index * (-2.0 * math.log(10000.0) / values.shape[1]))
    angles = inverse[:, None] * places[None, :]
    cosine = jnp.cos(angles)[None]
    sine_part = jnp.sin(angles)[None]
    leading = values[:, :half]
    trailing = values[:, half:]
    return jnp.concatenate(
        [leading * cosine - trailing * sine_part, trailing * cosine + leading * sine_part], axis=1
    )


def softmax_part(query_block, keys, values, mask, scale):
    scores = (
        jnp.einsum("hdq,hdk->hqk", query_block, keys, preferred_element_type=jnp.float32) * scale
    )
    scores = jnp.where(mask[None], scores, masked_score)
    highest = jnp.max(scores, axis=2)
    expo = jnp.where(mask[None], jnp.exp(scores - highest[:, :, None]), 0.0)
    total = jnp.sum(expo, axis=2)
    mixed = jnp.einsum("hqk,hdk->hdq", expo, values, precision=lax.Precision.HIGHEST)
    return (mixed, highest, total)


def fold_softmax(first, second):
    mixed_a, high_a, total_a = first
    mixed_b, high_b, total_b = second
    top = jnp.maximum(high_a, high_b)
    factor_a = jnp.exp(high_a - top)
    factor_b = jnp.exp(high_b - top)
    return (
        mixed_a * factor_a[:, None, :] + mixed_b * factor_b[:, None, :],
        top,
        total_a * factor_a + total_b * factor_b,
    )


def unblock(parts):
    mixed, highest, total = parts
    heads_here = mixed.shape[1]
    mixed = jnp.transpose(mixed, (1, 2, 0, 3)).reshape(heads_here, mixed.shape[2], -1)
    highest = jnp.transpose(highest, (1, 0, 2)).reshape(heads_here, -1)
    total = jnp.transpose(total, (1, 0, 2)).reshape(heads_here, -1)
    return (mixed, highest, total)


def shards(
    vision, ln_gain, merge_proj, image_slot, text, rms_gain, wqkv, pcache, block_table, cache_len
):
    local = vision.shape[1]
    groups = vision.shape[2]
    floats = vision.astype(jnp.float32)
    totals, squares = lax.psum((jnp.sum(floats, axis=1), jnp.sum(floats * floats, axis=1)), "head")
    average = totals / D
    spread = squares / D - average * average
    normed_vision = (
        (floats - average[:, None, :])
        * lax.rsqrt(spread + 1e-06)[:, None, :]
        * ln_gain[None, :, None]
    ).astype(jnp.bfloat16)
    partial_rows = jnp.einsum(
        "tcd,tcg->dg", merge_proj, normed_vision, preferred_element_type=jnp.float32
    )
    merged_columns = lax.psum_scatter(partial_rows, "head", scatter_dimension=0, tiled=True).astype(
        jnp.bfloat16
    )
    merged = jnp.transpose(merged_columns)
    devices = lax.axis_size("blk")
    here = lax.axis_index("blk")
    rows_here = text.shape[1]
    pieces = image_slot.shape[0]
    piece_rows = groups // pieces
    lines = jnp.arange(rows_here, dtype=jnp.int32)
    offsets = jnp.arange(piece_rows, dtype=jnp.int32)
    target = image_slot // rows_here
    within = image_slot % rows_here
    select = target[None, :] == jnp.arange(devices, dtype=jnp.int32)[:, None]
    outbound = (
        jnp.dot(
            select.astype(jnp.bfloat16),
            merged.reshape(pieces, piece_rows * local),
            preferred_element_type=jnp.float32,
        )
        .astype(jnp.bfloat16)
        .reshape(devices, piece_rows, local)
    )
    starts = jnp.sum(jnp.where(select, within[None, :] + 1, 0), axis=1) - 1
    arrived, arrived_start = (
        lax.all_to_all(outbound, "blk", split_axis=0, concat_axis=0, tiled=True),
        lax.all_to_all(starts, "blk", split_axis=0, concat_axis=0, tiled=True),
    )
    row_ids = (arrived_start[:, None] + offsets[None, :]).reshape(-1)
    present = jnp.repeat(arrived_start >= 0, piece_rows)
    hits = (row_ids[:, None] == lines[None, :]) & present[:, None]
    placed_rows = jnp.einsum(
        "kl,kr->lr",
        arrived.reshape(devices * piece_rows, local),
        hits.astype(jnp.bfloat16),
        preferred_element_type=jnp.float32,
    ).astype(jnp.bfloat16)
    covered = jnp.any(hits, axis=0)
    placed = jnp.where(covered[None, :], placed_rows, text)
    row_floats = placed.astype(jnp.float32)
    square_sums = lax.psum(jnp.sum(row_floats * row_floats, axis=0), "head")
    gain_here = lax.dynamic_slice_in_dim(rms_gain, lax.axis_index("head") * local, local)
    normed = (row_floats * lax.rsqrt(square_sums / D + 1e-06)[None, :] * gain_here[:, None]).astype(
        jnp.bfloat16
    )
    projected = jnp.einsum(
        "jod,dr->jor",
        wqkv,
        lax.all_gather(normed, "head", axis=0, tiled=True),
        preferred_element_type=jnp.float32,
    )
    heads_here = local // HD
    projected = projected.reshape(3, heads_here, HD, rows_here)
    places = (cache_len[0] + lines).astype(jnp.float32)
    queries = rotary_columns(projected[0], places).astype(jnp.bfloat16)
    new_keys = rotary_columns(projected[1], places).astype(jnp.bfloat16)
    new_values = projected[2].astype(jnp.bfloat16)
    new_cache = jnp.stack(
        [new_keys.reshape(local, rows_here), new_values.reshape(local, rows_here)], axis=0
    )
    block_len = BS
    owned = pcache.shape[2] // block_len
    paged = pcache.reshape(2, local, owned, block_len)
    requests = block_table.shape[0]
    table_width = block_table.shape[1]
    slots_each = table_width // devices
    block_ids = here * owned + jnp.arange(owned, dtype=jnp.int32)
    matches = block_table[None, :, :] == block_ids[:, None, None]
    found = jnp.any(matches, axis=2)
    in_use = jnp.any(found, axis=1)
    owner = jnp.sum(jnp.where(found, jnp.arange(requests, dtype=jnp.int32)[None, :], 0), axis=1)
    logical = jnp.sum(
        jnp.where(matches, jnp.arange(table_width, dtype=jnp.int32)[None, None, :], 0), axis=(1, 2)
    )
    counter = jnp.arange(owned, dtype=jnp.int32)
    earlier = (
        (owner[:, None] == owner[None, :]) & in_use[None, :] & (counter[None, :] < counter[:, None])
    )
    standing = jnp.sum(earlier.astype(jnp.int32), axis=1)
    within_block = jnp.arange(block_len, dtype=jnp.int32)
    block_rows = min(rows_here, 512)
    count_blocks = rows_here // block_rows
    scale = HD ** (-0.5)
    query_blocks = jnp.transpose(
        queries.reshape(heads_here, HD, count_blocks, block_rows), (2, 0, 1, 3)
    )
    first_rows = jnp.arange(count_blocks, dtype=jnp.int32) * block_rows
    destination = owner * slots_each + standing
    routing = (destination[None, :] == jnp.arange(table_width, dtype=jnp.int32)[:, None]) & in_use[
        None, :
    ]
    outgoing = jnp.einsum(
        "wo,cfob->cfwb", routing.astype(jnp.bfloat16), paged, preferred_element_type=jnp.float32
    ).astype(jnp.bfloat16)
    outgoing = outgoing.reshape(2, local, table_width * block_len)
    labels = jnp.sum(jnp.where(routing, logical[None, :] + 1, 0), axis=1) - 1
    labels = labels.reshape(1, 1, table_width)
    blocks_in, labels_in = (
        lax.all_to_all(outgoing, "blk", split_axis=2, concat_axis=2, tiled=True),
        lax.all_to_all(labels, "blk", split_axis=2, concat_axis=2, tiled=True),
    )
    cached_keys = blocks_in[0].reshape(heads_here, HD, -1)
    cached_values = blocks_in[1].reshape(heads_here, HD, -1).astype(jnp.float32)
    label_flat = labels_in.reshape(-1)
    key_places = label_flat[:, None] * block_len + within_block[None, :]
    live = ((label_flat[:, None] >= 0) & (key_places < cache_len[0])).reshape(-1)
    old_mask = jnp.broadcast_to(live[None, :], (block_rows, live.shape[0]))
    new_values_f = new_values.astype(jnp.float32)

    def attend(inputs):
        query_block, first_row = inputs
        causal = (first_row + jnp.arange(block_rows, dtype=jnp.int32))[:, None] >= lines[None, :]
        old_part = softmax_part(query_block, cached_keys, cached_values, old_mask, scale)
        own_part = softmax_part(query_block, new_keys, new_values_f, causal, scale)
        return fold_softmax(old_part, own_part)

    mixed, highest, total = unblock(lax.map(attend, (query_blocks, first_rows)))
    attended = (mixed / total[:, None, :]).astype(jnp.bfloat16).reshape(local, rows_here)
    return (attended, new_cache)


def solution(mesh):
    in_specs = (
        P(None, "head", "blk"),
        P("head"),
        P(None, "head", None),
        P("blk"),
        P("head", "blk"),
        P(),
        P(None, "head", None),
        P(None, "head", "blk"),
        P(),
        P("blk"),
    )
    out_specs = (P("head", "blk"), P(None, "head", "blk"))
    return jax.shard_map(shards, mesh=mesh, in_specs=in_specs, out_specs=out_specs, check_vma=False)
```

profile of v0, /device:TPU:1, one launch (start us, length us, event | category | flops | bytes accessed | tf_op | source)
XLA Modules:
  0.0 288.2 jit_solution(1287686254156349032)
XLA Ops:
  7.2 1.1 convert_reduce_fusion
  8.3 20.3 %all-reduce = (f32[4,128]{1,0:T(4,128)S(1)}, f32[4,128]{1,0:T(4,128)S(1)}) all-reduce(f32[4,128]{1,0:T(4,128)S(1)} %get-tuple-element.23, f32[4,128]{1,0:T(4,128)S(1)} %get-tuple-element.22), channel_id=1, replica_groups=mesh['head'=8,'blk'=64] {'head'}, use_global_device_ids=true, to_apply=%region_11.12 | all-reduce | flops 1024 | bytes 8192 | tf_op jit(solution)/shard_map/psum | solution.py:67
  28.6 1.5 convolution_bitcast_fusion
  30.2 1.1 copy.49
  31.5 0.7 copy.44
  32.2 14.5 %all-to-all-start.2 = ((s32[64,1,1]{2,1,0:T(1,128)}), s32[64,1,1]{2,1,0:T(1,128)S(1)}, u32[]{:S(2)}, u32[]{:S(2)}) async-start(s32[64,1,1]{2,1,0:T(1,128)} %copy.44), calls=%async_computation.2 | async-start | bytes 65536 | tf_op jit(solution)/shard_map/all_to_all | solution.py:104
  46.8 2.4 compare_reduce_fusion
  49.2 0.2 convert_reduce_fusion.1
  49.4 1.4 fusion.8
  50.8 0.1 select_reduce_fusion
  50.9 0.7 copy.43
  51.7 3.7 %copy.38 = bf16[2,176,2048]{1,2,0:T(8,128)(2,1)} copy(bf16[2,176,2048]{2,1,0:T(8,128)(2,1)} %param.17) | data formatting | bytes 2883584 | tf_op args[7]
  55.4 13.9 %reduce-scatter.4.cloned.1.call-done = f32[176,128]{1,0:T(8,128)} async-done(((f32[1408,128]{1,0:T(8,128)}), f32[176,128]{1,0:T(8,128)}) %reduce-scatter.4.cloned.1.call-update) | async-done | bytes 90128
  69.2 1.0 copy.50
  70.2 0.1 reshape.265
  70.4 14.6 %all-to-all-start.1 = ((s32[1,1,128]{1,0,2:T(1,128)}), s32[1,1,128]{1,0,2:T(1,128)S(1)}, u32[]{:S(2)}, u32[]{:S(2)}) async-start(s32[1,1,128]{1,0,2:T(1,128)} %copy.43), calls=%async_computation.1 | async-start | bytes 131072 | tf_op jit(solution)/shard_map/all_to_all | solution.py:177
  85.0 0.3 convolution_convert_fusion.1
  85.3 0.8 reshape.266
  86.1 8.7 %all-to-all-done.1 = s32[1,1,128]{1,0,2:T(1,128)S(1)} async-done(((s32[1,1,128]{1,0,2:T(1,128)}), s32[1,1,128]{1,0,2:T(1,128)S(1)}, u32[]{:S(2)}, u32[]{:S(2)}) %all-to-all-start.1) | async-done | bytes 544 | tf_op jit(solution)/shard_map/all_to_all | solution.py:177
  94.8 4.4 %all-to-all-start.3 = ((bf16[64,4,176]{2,1,0:T(4,128)(2,1)}), bf16[64,4,176]{2,1,0:T(4,128)(2,1)S(1)}, u32[]{:S(2)}, u32[]{:S(2)}) async-start(bf16[64,4,176]{2,1,0:T(4,128)(2,1)} %reshape.266), calls=%async_computation.3 | async-start | bytes 262144 | tf_op jit(solution)/shard_map/all_to_all | solution.py:103
  99.2 4.9 %convert_bitcast_fusion = bf16[2,176,128,32]{2,1,3,0:T(8,128)(2,1)} fusion(bf16[2,176,64,32]{1,3,2,0:T(8,128)(2,1)} %bitcast.47, s32[64]{0:T(128)S(1)} %get-tuple-element.61, pred[64]{0:T(512)(128)(4,1)S(1)} %get-tuple-element.24), kind=kOutput, calls=%fused_computation.13 | convolution fusion | flops 186007552 | bytes 4325696 | tf_op jit(solution)/shard_map/wo,cfob->cfwb/dot_general | solution.py:169
  104.1 7.7 %copy.40 = bf16[2,176,128,32]{1,3,2,0:T(8,128)(2,1)} copy(bf16[2,176,128,32]{2,1,3,0:T(8,128)(2,1)} %convert_bitcast_fusion) | data formatting | bytes 5767168 | tf_op jit(solution)/shard_map/convert_element_type | solution.py:171
  111.8 10.1 %copy.41 = bf16[2,176,4096]{1,0,2:T(2,128)(2,1)} copy(bf16[2,176,4096]{1,2,0:T(8,128)(2,1)} %bitcast.46) | data formatting | bytes 5767168 | tf_op jit(solution)/shard_map/reshape | solution.py:172
  121.9 10.8 %all-to-all-start = ((bf16[2,176,4096]{1,0,2:T(2,128)(2,1)}), bf16[2,176,4096]{1,0,2:T(2,128)(2,1)}, u32[]{:S(2)}, u32[]{:S(2)}) async-start(bf16[2,176,4096]{1,0,2:T(2,128)(2,1)} %copy.41), calls=%async_computation | async-start | bytes 8388608 | tf_op jit(solution)/shard_map/all_to_all | solution.py:176
  132.7 0.8 dynamic_slice.9
  133.5 1.2 reduce.3
  134.8 0.1 and.66
  135.1 0.2 fusion.32
  135.4 0.4 multiply_reduce_fusion
  135.7 13.1 %psum.23 = f32[512]{0:T(512)S(1)} all-reduce(f32[512]{0:T(512)S(1)} %get-tuple-element.55), channel_id=1, replica_groups=mesh['head'=8,'blk'=64] {'head'}, use_global_device_ids=true, to_apply=%region_14.15 | all-reduce | flops 512 | bytes 4096 | tf_op jit(solution)/shard_map/psum | solution.py:118
  148.9 0.8 multiply_convert_fusion
  150.5 0.4 multiply_cosine_fusion
  150.9 2.4 multiply_reduce_fusion.1
  153.2 2.4 compare_reduce_fusion.2
  155.8 34.9 %all-gather.2.cloned.1.call-done = bf16[1408,512]{1,0:T(8,128)(2,1)} async-done(((bf16[176,512]{1,0:T(8,128)(2,1)}), bf16[1408,512]{1,0:T(8,128)(2,1)}) %all-gather.2.cloned.1.call-update) | async-done | bytes 1441808 | tf_op jit(solution)/shard_map/all_gather | solution.py:126
  190.7 2.8 fusion.15
  193.7 0.8 pad_maximum_fusion
  194.6 0.6 fusion.10
  195.3 1.3 copy-done.1
  196.6 0.6 fusion.11
  197.2 31.4 %all-to-all-done = bf16[2,176,4096]{1,0,2:T(2,128)(2,1)} async-done(((bf16[2,176,4096]{1,0,2:T(2,128)(2,1)}), bf16[2,176,4096]{1,0,2:T(2,128)(2,1)}, u32[]{:S(2)}, u32[]{:S(2)}) %all-to-all-start) | async-done | bytes 2883616 | tf_op jit(solution)/shard_map/all_to_all | solution.py:176
  228.6 9.8 %fusion.66 = (bf16[1,176,4096]{1,0,2:T(2,128)(2,1)}, bf16[1,176,4096]{1,0,2:T(2,128)(2,1)}) fusion(bf16[2,176,4096]{1,0,2:T(2,128)(2,1)} %all-to-all-done), kind=kLoop, calls=%fused_computation.118 | loop fusion | bytes 5767168 | tf_op jit(solution)/shard_map/slice | solution.py:180
  238.3 9.6 %copy.42 = bf16[1,176,4096]{2,1,0:T(8,128)(2,1)} copy(bf16[1,176,4096]{1,0,2:T(2,128)(2,1)} %get-tuple-element.41) | data formatting | bytes 2883584 | tf_op jit(solution)/shard_map/slice | solution.py:180
  247.9 9.8 %copy.45 = bf16[1,176,4096]{2,1,0:T(8,128)(2,1)S(1)} copy(bf16[1,176,4096]{1,0,2:T(2,128)(2,1)} %get-tuple-element.42) | data formatting | bytes 2883584 | tf_op jit(solution)/shard_map/slice | solution.py:179
  257.7 3.7 %fusion = (f32[2,512]{1,0:T(2,128)S(1)}, f32[2,512,4096]{2,1,0:T(8,128)S(1)}) fusion(pred[4096]{0:T(1024)(128)(4,1)S(1)} %and.63, bf16[2,88,4096]{2,1,0:T(8,128)(2,1)S(1)} %bitcast.48, bf16[2,44,512]{2,1,0:T(8,128)(2,1)} %copy-done.8, bf16[2,44,512]{2,1,0:T(8,128)(2,1)S(1)} %get-tuple-element.45), kind=kOutput, calls=%fused_computation.2 | convolution fusion | flops 751139840 | bytes 18407424 | tf_op jit(solution)/shard_map/while/body/eval_jaxpr/hdq,hdk->hqk/dot_general | solution.py:29
  261.5 5.1 %fusion.1 = f32[2,512]{1,0:T(2,128)S(1)} fusion(f32[2,512,4096]{2,1,0:T(8,128)S(1)} %get-tuple-element.60, f32[2,512]{1,0:T(2,128)S(1)} %get-tuple-element.59, pred[4096]{0:T(1024)(128)(4,1)S(1)} %and.63), kind=kLoop, calls=%fused_computation.3 | loop fusion | flops 20970496 | bytes 16789504 | tf_op jit(solution)/shard_map/while/body/eval_jaxpr/reduce_sum | solution.py:34
  266.6 1.5 fusion.20
  268.1 13.2 %fusion.29 = bf16[2,88,512]{2,1,0:T(8,128)(2,1)} fusion(f32[2,88,512]{2,1,0:T(8,128)S(1)} %fusion.20, bf16[2,88,4096]{2,1,0:T(8,128)(2,1)S(1)} %bitcast.51, f32[2,512,4096]{2,1,0:T(8,128)S(1)} %get-tuple-element.60, f32[2,512]{1,0:T(2,128)S(1)} %get-tuple-element.59, pred[4096]{0:T(1024)(128)(4,1)S(1)} %and.63, f32[2,512]{1,0:T(2,128)S(1)} %get-tuple-element.28, ...), kind=kOutput, calls=%fused_computation.39 | convolution fusion | flops 4446322688 | bytes 18776064 | tf_op jit(solution)/shard_map/while/body/eval_jaxpr/hqk,hdk->hdq/dot_general | solution.py:35
  (54 shorter events, 1.4 us)
Async XLA Ops:
  7.2 21.5 %copy-start = (bf16[4,176,1408]{2,1,0:T(8,128)(2,1)S(1)}, bf16[4,176,1408]{2,1,0:T(8,128)(2,1)}, u32[]{:S(2)}) copy-start(bf16[4,176,1408]{2,1,0:T(8,128)(2,1)} %param.12) | copy-start | bytes 5947396
  7.2 62.0 %reduce-scatter.4.cloned.1.call-start = ((), (), s32[]{:S(2)}) async-start(), calls=%async_computation.6 | async-start | bytes 811008
  28.6 2.7 copy-start.11
  28.6 18.1 %copy-start.9 = (s32[64,128]{1,0:T(8,128)S(1)}, s32[64,128]{1,0:T(8,128)}, u32[]{:S(2)}) copy-start(s32[64,128]{1,0:T(8,128)} %param.18) | copy-start | bytes 98308
  32.2 38.2 %all-to-all-start.2 = ((s32[64,1,1]{2,1,0:T(1,128)}), s32[64,1,1]{2,1,0:T(1,128)S(1)}, u32[]{:S(2)}, u32[]{:S(2)}) async-start(s32[64,1,1]{2,1,0:T(1,128)} %copy.44), calls=%async_computation.2 | async-start | bytes 65536 | tf_op jit(solution)/shard_map/all_to_all | solution.py:104
  70.4 24.4 %all-to-all-start.1 = ((s32[1,1,128]{1,0,2:T(1,128)}), s32[1,1,128]{1,0,2:T(1,128)S(1)}, u32[]{:S(2)}, u32[]{:S(2)}) async-start(s32[1,1,128]{1,0,2:T(1,128)} %copy.43), calls=%async_computation.1 | async-start | bytes 131072 | tf_op jit(solution)/shard_map/all_to_all | solution.py:177
  94.8 27.1 %all-to-all-start.3 = ((bf16[64,4,176]{2,1,0:T(4,128)(2,1)}), bf16[64,4,176]{2,1,0:T(4,128)(2,1)S(1)}, u32[]{:S(2)}, u32[]{:S(2)}) async-start(bf16[64,4,176]{2,1,0:T(4,128)(2,1)} %reshape.266), calls=%async_computation.3 | async-start | bytes 262144 | tf_op jit(solution)/shard_map/all_to_all | solution.py:103
  121.9 13.5 %copy-start.10 = (bf16[176,512]{1,0:T(8,128)(2,1)S(1)}, bf16[176,512]{1,0:T(8,128)(2,1)}, u32[]{:S(2)}) copy-start(bf16[176,512]{1,0:T(8,128)(2,1)} %param.14) | copy-start | bytes 540676
  121.9 106.7 %all-to-all-start = ((bf16[2,176,4096]{1,0,2:T(2,128)(2,1)}), bf16[2,176,4096]{1,0,2:T(2,128)(2,1)}, u32[]{:S(2)}, u32[]{:S(2)}) async-start(bf16[2,176,4096]{1,0,2:T(2,128)(2,1)} %copy.41), calls=%async_computation | async-start | bytes 8388608 | tf_op jit(solution)/shard_map/all_to_all | solution.py:176
  132.7 58.0 %all-gather.2.cloned.1.call-start = ((), (), s32[]{:S(2)}) async-start(), calls=%async_computation.5 | async-start | bytes 1622016 | tf_op jit(solution)/shard_map/all_gather | solution.py:126
  150.5 44.8 %copy-start.4 = (pred[512,512]{0,1:T(8,128)(4,1)}, pred[512,512]{0,1:T(8,128)(4,1)S(1)}, u32[]{:S(2)}) copy-start(pred[512,512]{0,1:T(8,128)(4,1)S(1)} %iota_compare_fusion) | copy-start | bytes 786436
  193.6 1.0 copy-start.6
  194.6 2.6 copy-start.8
  195.2 1.4 copy-start.1
  261.4 5.2 %copy-start.2 = (f32[2,512,512]{1,2,0:T(8,128)S(1)}, f32[2,512,512]{1,2,0:T(8,128)}, u32[]{:S(2)}) copy-start(f32[2,512,512]{1,2,0:T(8,128)} %copy-done.1) | copy-start | bytes 6291460
  261.5 5.2 %copy-start.5 = (pred[512,512]{0,1:T(8,128)(4,1)S(1)}, pred[512,512]{0,1:T(8,128)(4,1)}, u32[]{:S(2)}) copy-start(pred[512,512]{0,1:T(8,128)(4,1)} %copy-done.4) | copy-start | bytes 786436
  261.5 5.2 %copy-start.7 = (bf16[1,176,512]{2,1,0:T(8,128)(2,1)S(1)}, bf16[1,176,512]{2,1,0:T(8,128)(2,1)}, u32[]{:S(2)}) copy-start(bf16[1,176,512]{2,1,0:T(8,128)(2,1)} %copy-done.6) | copy-start | bytes 540676
  266.6 1.5 copy-start.3
Sparse Core Ops, SparseCore 0:
  31.5 37.7 reduce-scatter.3
  149.8 40.8 all-gather.1
where the time goes:
time: 290 us; the launch traced here: 288 us
  waiting for transfers between devices  88.9 us (31%)
  local copies, waits for them, and re-layouts  57.9 us (20%)
  starting transfers between devices  44.4 us (15%)
  blocking collectives  33.4 us (12%)
  matrix products  28.9 us (10%)
  other arithmetic  19.6 us (7%)
  between operations  15.1 us (5%)
    all_gather x1, waiting for transfers between devices, shards(): lax.all_gather(normed, 'head', axis=0, tiled=True)  34.9 us
    all_to_all x1, waiting for transfers between devices, shards(): lax.all_to_all(outgoing, 'blk', split_axis=2, concat_axis=2, tiled=True)  31.4 us
    psum x1, blocking collectives, shards(): lax.psum((jnp.sum(floats, axis=1), jnp.sum(floats * floats, axis=1)), 'he...  20.3 us
    slice x2, local copies, waits for them, and re-layouts, shards(): cached_values = blocks_in[1].reshape(heads_here, HD, -1).astype(jnp.float32)  19.4 us
    dot_general x2, matrix products, softmax_part(): jnp.einsum('hqk,hdk->hdq', expo, values, precision=lax.Precision.HIGHEST)  14.7 us
    all_to_all x1, starting transfers between devices, shards(): lax.all_to_all(labels, 'blk', split_axis=2, concat_axis=2, tiled=True)  14.6 us
    all_to_all x1, starting transfers between devices, shards(): lax.all_to_all(starts, 'blk', split_axis=0, concat_axis=0, tiled=True)  14.5 us
    unnamed x3, waiting for transfers between devices  13.9 us
  transfers between devices with their start and end apart: 6, of which 4 were waited for; matrix products, arithmetic and copies ran while one was open for 17% of the time, Pallas kernels for 0%

commit v1 on v0

--- a/solution.py
+++ b/solution.py
@@ -120,12 +120,39 @@
     normed = (row_floats * lax.rsqrt(square_sums / D + 1e-06)[None, :] * gain_here[:, None]).astype(
         jnp.bfloat16
     )
+    back = lax.axis_size("head")
+    found_now = lax.axis_index("head")
+    then, reached, v_next = (back, found_now, normed.shape[0])
+    entries = [(m, (m + 1) % then) for m in range(then)]
+    seen = [(m, (m - 1) % then) for m in range(then)]
+    x_new = then // 2
+    prior = everything = normed
     projected = jnp.einsum(
         "jod,dr->jor",
-        wqkv,
-        lax.all_gather(normed, "head", axis=0, tiled=True),
+        lax.dynamic_slice_in_dim(wqkv, reached * v_next, normed.shape[0], axis=2),
+        normed,
         preferred_element_type=jnp.float32,
     )
+    for c in range(1, x_new + 1):
+        prior = lax.ppermute(prior, "head", entries)
+        if c < then - x_new:
+            everything = lax.ppermute(everything, "head", seen)
+            inter = jnp.einsum(
+                "jod,dr->jor",
+                lax.dynamic_slice_in_dim(
+                    wqkv, (reached + c) % then * v_next, everything.shape[0], axis=2
+                ),
+                everything,
+                preferred_element_type=jnp.float32,
+            )
+            projected = projected + inter
+        n_now = jnp.einsum(
+            "jod,dr->jor",
+            lax.dynamic_slice_in_dim(wqkv, (reached - c) % then * v_next, prior.shape[0], axis=2),
+            prior,
+            preferred_element_type=jnp.float32,
+        )
+        projected = projected + n_now
     heads_here = local // HD
     projected = projected.reshape(3, heads_here, HD, rows_here)
     places = (cache_len[0] + lines).astype(jnp.float32)

time: 290 us -> 283 us (0.976)
  waiting for transfers between devices: 88.9 us -> 70.7 us
  starting transfers between devices: 44.4 us -> 58.3 us
    all_gather x1 -> x0, waiting for transfers between devices: 34.9 us -> none  [shards(): lax.all_gather(normed, 'head', axis=0, tiled=True)]
    ppermute x0 -> x7, starting transfers between devices: none -> 21.4 us  [the longest x3 13.3 us: shards(): everything = lax.ppermute(everything, 'head', seen)]
    all_to_all x1, waiting for transfers between devices: 0.01 us -> 10.4 us  [shards(): lax.all_to_all(outbound, 'blk', split_axis=0, concat_axis=0, tiled=True)]
    unnamed x3 -> x2, waiting for transfers between devices: 13.9 us -> 5.51 us
    all_to_all x1, waiting for transfers between devices: 31.4 us -> 38.7 us  [shards(): lax.all_to_all(outgoing, 'blk', split_axis=2, concat_axis=2, tiled=True)]
    ppermute x0 -> x7, waiting for transfers between devices: none -> 7.31 us  [the longest x4 7.3 us: shards(): prior = lax.ppermute(prior, 'head', entries)]
    all_to_all x1, starting transfers between devices: 10.8 us -> 5.61 us  [shards(): lax.all_to_all(outgoing, 'blk', split_axis=2, concat_axis=2, tiled=True)]
    all_to_all x1, starting transfers between devices: 14.5 us -> 11.6 us  [shards(): lax.all_to_all(starts, 'blk', split_axis=0, concat_axis=0, tiled=True)]
  transfers between devices with their start and end apart: 6 -> 12, of which waited for: 4 -> 8; matrix products, arithmetic and copies ran while one was open for 17% -> 18% of each run, Pallas kernels for 0% -> 0%
where the time goes in v1:
time: 283 us; the launch traced here: 282 us
  waiting for transfers between devices  70.7 us (25%)
  starting transfers between devices  58.3 us (21%)
  local copies, waits for them, and re-layouts  57.2 us (20%)
  blocking collectives  32.8 us (12%)
  matrix products  28.1 us (10%)
  other arithmetic  19.4 us (7%)
  between operations  15.3 us (5%)
    all_to_all x1, waiting for transfers between devices, shards(): lax.all_to_all(outgoing, 'blk', split_axis=2, concat_axis=2, tiled=True)  38.7 us
    psum x1, blocking collectives, shards(): lax.psum((jnp.sum(floats, axis=1), jnp.sum(floats * floats, axis=1)), 'he...  19.7 us
    slice x2, local copies, waits for them, and re-layouts, shards(): cached_values = blocks_in[1].reshape(heads_here, HD, -1).astype(jnp.float32)  19.6 us
    all_to_all x1, starting transfers between devices, shards(): lax.all_to_all(labels, 'blk', split_axis=2, concat_axis=2, tiled=True)  15.2 us
    dot_general x2, matrix products, softmax_part(): jnp.einsum('hqk,hdk->hdq', expo, values, precision=lax.Precision.HIGHEST)  14.7 us
    ppermute x3, starting transfers between devices, shards(): everything = lax.ppermute(everything, 'head', seen)  13.3 us
    psum x1, blocking collectives, shards(): square_sums = lax.psum(jnp.sum(row_floats * row_floats, axis=0), 'head')  13.1 us
    all_to_all x1, starting transfers between devices, shards(): lax.all_to_all(starts, 'blk', split_axis=0, concat_axis=0, tiled=True)  11.6 us
  transfers between devices with their start and end apart: 12, of which 8 were waited for; matrix products, arithmetic and copies ran while one was open for 18% of the time, Pallas kernels for 0%

profile of v1, /device:TPU:1, one launch (start us, length us, event | category | flops | bytes accessed | tf_op | source)
XLA Modules:
  0.0 281.8 jit_solution(16765341290492751347)
XLA Ops:
  7.2 0.8 fusion.79
  8.1 0.7 copy.44
  8.8 11.6 %all-to-all-start.2 = ((s32[64,1,1]{2,1,0:T(1,128)}), s32[64,1,1]{2,1,0:T(1,128)S(1)}, u32[]{:S(2)}, u32[]{:S(2)}) async-start(s32[64,1,1]{2,1,0:T(1,128)} %copy.44), calls=%async_computation.2 | async-start | bytes 65536 | tf_op jit(solution)/shard_map/all_to_all | solution.py:104
  20.5 1.0 convert_reduce_fusion
  21.5 19.7 %all-reduce = (f32[4,128]{1,0:T(4,128)S(1)}, f32[4,128]{1,0:T(4,128)S(1)}) all-reduce(f32[4,128]{1,0:T(4,128)S(1)} %get-tuple-element.23, f32[4,128]{1,0:T(4,128)S(1)} %get-tuple-element.22), channel_id=1, replica_groups=mesh['head'=8,'blk'=64] {'head'}, use_global_device_ids=true, to_apply=%region_11.12 | all-reduce | flops 1024 | bytes 8192 | tf_op jit(solution)/shard_map/psum | solution.py:67
  41.2 1.5 convolution_bitcast_fusion
  42.7 1.2 copy.49
  44.3 2.4 copy.38
  46.7 2.4 compare_reduce_fusion
  49.4 1.4 fusion.8
  50.9 4.9 %convert_bitcast_fusion = bf16[2,176,128,32]{2,1,3,0:T(8,128)(2,1)} fusion(bf16[2,176,64,32]{1,3,2,0:T(8,128)(2,1)} %bitcast.63, s32[64]{0:T(128)S(1)} %get-tuple-element.61, pred[64]{0:T(512)(128)(4,1)S(1)} %get-tuple-element.24), kind=kOutput, calls=%fused_computation.13 | convolution fusion | flops 186007552 | bytes 4325696 | tf_op jit(solution)/shard_map/wo,cfob->cfwb/dot_general | solution.py:196
  56.5 0.7 copy.43
  57.2 7.6 %copy.40 = bf16[2,176,128,32]{1,3,2,0:T(8,128)(2,1)} copy(bf16[2,176,128,32]{2,1,3,0:T(8,128)(2,1)} %convert_bitcast_fusion) | data formatting | bytes 5767168 | tf_op jit(solution)/shard_map/convert_element_type | solution.py:198
  64.8 10.1 %copy.41 = bf16[2,176,4096]{1,0,2:T(2,128)(2,1)} copy(bf16[2,176,4096]{1,2,0:T(8,128)(2,1)} %bitcast.62) | data formatting | bytes 5767168 | tf_op jit(solution)/shard_map/reshape | solution.py:199
  74.9 5.5 %reduce-scatter.4.cloned.1.call-done = f32[176,128]{1,0:T(8,128)} async-done(((f32[1408,128]{1,0:T(8,128)}), f32[176,128]{1,0:T(8,128)}) %reduce-scatter.4.cloned.1.call-update) | async-done | bytes 90128
  80.4 1.0 copy.50
  81.6 15.2 %all-to-all-start.1 = ((s32[1,1,128]{1,0,2:T(1,128)}), s32[1,1,128]{1,0,2:T(1,128)S(1)}, u32[]{:S(2)}, u32[]{:S(2)}) async-start(s32[1,1,128]{1,0,2:T(1,128)} %copy.43), calls=%async_computation.1 | async-start | bytes 131072 | tf_op jit(solution)/shard_map/all_to_all | solution.py:204
  97.1 0.8 reshape.266
  97.9 8.7 %all-to-all-done.1 = s32[1,1,128]{1,0,2:T(1,128)S(1)} async-done(((s32[1,1,128]{1,0,2:T(1,128)}), s32[1,1,128]{1,0,2:T(1,128)S(1)}, u32[]{:S(2)}, u32[]{:S(2)}) %all-to-all-start.1) | async-done | bytes 544 | tf_op jit(solution)/shard_map/all_to_all | solution.py:204
  106.6 4.4 %all-to-all-start.3 = ((bf16[64,4,176]{2,1,0:T(4,128)(2,1)}), bf16[64,4,176]{2,1,0:T(4,128)(2,1)S(1)}, u32[]{:S(2)}, u32[]{:S(2)}) async-start(bf16[64,4,176]{2,1,0:T(4,128)(2,1)} %reshape.266), calls=%async_computation.3 | async-start | bytes 262144 | tf_op jit(solution)/shard_map/all_to_all | solution.py:103
  111.1 10.4 %all-to-all-done.3 = bf16[64,4,176]{2,1,0:T(4,128)(2,1)S(1)} async-done(((bf16[64,4,176]{2,1,0:T(4,128)(2,1)}), bf16[64,4,176]{2,1,0:T(4,128)(2,1)S(1)}, u32[]{:S(2)}, u32[]{:S(2)}) %all-to-all-start.3) | async-done | bytes 90144 | tf_op jit(solution)/shard_map/all_to_all | solution.py:103
  121.5 5.6 %all-to-all-start = ((bf16[2,176,4096]{1,0,2:T(2,128)(2,1)}), bf16[2,176,4096]{1,0,2:T(2,128)(2,1)}, u32[]{:S(2)}, u32[]{:S(2)}) async-start(bf16[2,176,4096]{1,0,2:T(2,128)(2,1)} %copy.41), calls=%async_computation | async-start | bytes 8388608 | tf_op jit(solution)/shard_map/all_to_all | solution.py:203
  127.7 0.8 dynamic_slice.34
  128.6 1.2 reduce.3
  130.4 2.4 multiply_reduce_fusion.1
  132.7 2.4 compare_reduce_fusion.2
  135.8 13.1 %psum.23 = f32[512]{0:T(512)S(1)} all-reduce(f32[512]{0:T(512)S(1)} %get-tuple-element.55), channel_id=1, replica_groups=mesh['head'=8,'blk'=64] {'head'}, use_global_device_ids=true, to_apply=%region_14.15 | all-reduce | flops 512 | bytes 4096 | tf_op jit(solution)/shard_map/psum | solution.py:118
  149.0 2.4 collective-permute-start.1
  151.4 4.1 %collective-permute-start = (bf16[176,512]{1,0:T(8,128)(2,1)S(1)}, bf16[176,512]{1,0:T(8,128)(2,1)S(1)}, u32[]{:S(2)}, u32[]{:S(2)}) collective-permute-start(bf16[176,512]{1,0:T(8,128)(2,1)S(1)} %multiply_convert_fusion), channel_id=1, source_target_pairs={{0,448},{64,0},{128,64},{192,128},{256,192},{320,256},{384,320},{4... | collective-permute-start | bytes 540680 | tf_op jit(solution)/shard_map/ppermute | solution.py:139
  155.9 1.0 collective-permute-done.1
  156.8 1.9 collective-permute-start.3
  158.7 4.6 %collective-permute-start.2 = (bf16[176,512]{1,0:T(8,128)(2,1)S(1)}, bf16[176,512]{1,0:T(8,128)(2,1)S(1)}, u32[]{:S(2)}, u32[]{:S(2)}) collective-permute-start(bf16[176,512]{1,0:T(8,128)(2,1)S(1)} %collective-permute-done), channel_id=1, source_target_pairs={{0,448},{64,0},{128,64},{192,128},{256,192},{320,256},{384,320},{4... | collective-permute-start | bytes 540680 | tf_op jit(solution)/shard_map/ppermute | solution.py:139
  164.7 1.9 collective-permute-start.5
  166.6 4.6 %collective-permute-start.4 = (bf16[176,512]{1,0:T(8,128)(2,1)S(1)}, bf16[176,512]{1,0:T(8,128)(2,1)S(1)}, u32[]{:S(2)}, u32[]{:S(2)}) collective-permute-start(bf16[176,512]{1,0:T(8,128)(2,1)S(1)} %collective-permute-done.2), channel_id=1, source_target_pairs={{0,448},{64,0},{128,64},{192,128},{256,192},{320,256},{384,320},{4... | collective-permute-start | bytes 540680 | tf_op jit(solution)/shard_map/ppermute | solution.py:139
  171.9 0.6 collective-permute-done.5
  172.5 1.9 collective-permute-start.6
  175.2 5.2 %collective-permute-done.6 = bf16[176,512]{1,0:T(8,128)(2,1)S(1)} collective-permute-done((bf16[176,512]{1,0:T(8,128)(2,1)S(1)}, bf16[176,512]{1,0:T(8,128)(2,1)S(1)}, u32[]{:S(2)}, u32[]{:S(2)}) %collective-permute-start.6) | collective-permute-done | bytes 180256 | tf_op jit(solution)/shard_map/ppermute | solution.py:137
  180.9 0.8 pad_maximum_fusion
  181.8 0.6 fusion.10
  182.4 1.4 copy-done.3
  184.4 38.7 %all-to-all-done = bf16[2,176,4096]{1,0,2:T(2,128)(2,1)} async-done(((bf16[2,176,4096]{1,0,2:T(2,128)(2,1)}), bf16[2,176,4096]{1,0,2:T(2,128)(2,1)}, u32[]{:S(2)}, u32[]{:S(2)}) %all-to-all-start) | async-done | bytes 2883616 | tf_op jit(solution)/shard_map/all_to_all | solution.py:203
  223.1 9.8 %fusion.90 = (bf16[1,176,4096]{1,0,2:T(2,128)(2,1)}, bf16[1,176,4096]{1,0,2:T(2,128)(2,1)}) fusion(bf16[2,176,4096]{1,0,2:T(2,128)(2,1)} %all-to-all-done), kind=kLoop, calls=%fused_computation.149 | loop fusion | bytes 5767168 | tf_op jit(solution)/shard_map/slice | solution.py:207
  232.9 9.8 %copy.42 = bf16[1,176,4096]{2,1,0:T(8,128)(2,1)S(1)} copy(bf16[1,176,4096]{1,0,2:T(2,128)(2,1)} %get-tuple-element.41) | data formatting | bytes 2883584 | tf_op jit(solution)/shard_map/slice | solution.py:207
  242.7 9.8 %copy.45 = bf16[1,176,4096]{2,1,0:T(8,128)(2,1)S(1)} copy(bf16[1,176,4096]{1,0,2:T(2,128)(2,1)} %get-tuple-element.42) | data formatting | bytes 2883584 | tf_op jit(solution)/shard_map/slice | solution.py:206
  252.5 2.8 %fusion = (f32[2,512]{1,0:T(2,128)S(1)}, f32[2,512,4096]{2,1,0:T(8,128)S(1)}) fusion(pred[4096]{0:T(1024)(128)(4,1)S(1)} %and.92, bf16[2,88,4096]{2,1,0:T(8,128)(2,1)S(1)} %bitcast.64, bf16[2,44,512]{2,1,0:T(8,128)(2,1)S(1)} %copy-done.9, bf16[2,44,512]{2,1,0:T(8,128)(2,1)S(1)} %get-tuple-element.45), kind=kOutput, calls=%fused_computation.2 | convolution fusion | flops 751139840 | bytes 18407424 | tf_op jit(solution)/shard_map/while/body/eval_jaxpr/hdq,hdk->hqk/dot_general | solution.py:29
  255.4 4.9 %fusion.1 = f32[2,512]{1,0:T(2,128)S(1)} fusion(f32[2,512,4096]{2,1,0:T(8,128)S(1)} %get-tuple-element.60, f32[2,512]{1,0:T(2,128)S(1)} %get-tuple-element.59, pred[4096]{0:T(1024)(128)(4,1)S(1)} %and.92), kind=kLoop, calls=%fused_computation.3 | loop fusion | flops 20970496 | bytes 16789504 | tf_op jit(solution)/shard_map/while/body/eval_jaxpr/reduce_sum | solution.py:34
  260.3 1.5 fusion.17
  261.8 13.2 %fusion.26 = bf16[2,88,512]{2,1,0:T(8,128)(2,1)} fusion(f32[2,88,512]{2,1,0:T(8,128)S(1)} %fusion.17, bf16[2,88,4096]{2,1,0:T(8,128)(2,1)S(1)} %bitcast.67, f32[2,512,4096]{2,1,0:T(8,128)S(1)} %get-tuple-element.60, f32[2,512]{1,0:T(2,128)S(1)} %get-tuple-element.59, pred[4096]{0:T(1024)(128)(4,1)S(1)} %and.92, f32[2,512]{1,0:T(2,128)S(1)} %get-tuple-element.28, ...), kind=kOutput, calls=%fused_computation.43 | convolution fusion | flops 4446322688 | bytes 18776064 | tf_op jit(solution)/shard_map/while/body/eval_jaxpr/hqk,hdk->hdq/dot_general | solution.py:35
  (72 shorter events, 7.6 us)
Async XLA Ops:
  7.2 34.0 %copy-start = (bf16[4,176,1408]{2,1,0:T(8,128)(2,1)S(1)}, bf16[4,176,1408]{2,1,0:T(8,128)(2,1)}, u32[]{:S(2)}) copy-start(bf16[4,176,1408]{2,1,0:T(8,128)(2,1)} %param.12) | copy-start | bytes 5947396
  8.8 72.8 %all-to-all-start.2 = ((s32[64,1,1]{2,1,0:T(1,128)}), s32[64,1,1]{2,1,0:T(1,128)S(1)}, u32[]{:S(2)}, u32[]{:S(2)}) async-start(s32[64,1,1]{2,1,0:T(1,128)} %copy.44), calls=%async_computation.2 | async-start | bytes 65536 | tf_op jit(solution)/shard_map/all_to_all | solution.py:104
  20.4 60.0 %reduce-scatter.4.cloned.1.call-start = ((), (), s32[]{:S(2)}) async-start(), calls=%async_computation.5 | async-start | bytes 811008
  42.7 1.6 copy-start.5
  43.9 2.8 %copy-start.10 = (s32[64,128]{1,0:T(8,128)S(1)}, s32[64,128]{1,0:T(8,128)}, u32[]{:S(2)}) copy-start(s32[64,128]{1,0:T(8,128)} %param.18) | copy-start | bytes 98308
  81.6 25.0 %all-to-all-start.1 = ((s32[1,1,128]{1,0,2:T(1,128)}), s32[1,1,128]{1,0,2:T(1,128)S(1)}, u32[]{:S(2)}, u32[]{:S(2)}) async-start(s32[1,1,128]{1,0,2:T(1,128)} %copy.43), calls=%async_computation.1 | async-start | bytes 131072 | tf_op jit(solution)/shard_map/all_to_all | solution.py:204
  106.6 14.9 %all-to-all-start.3 = ((bf16[64,4,176]{2,1,0:T(4,128)(2,1)}), bf16[64,4,176]{2,1,0:T(4,128)(2,1)S(1)}, u32[]{:S(2)}, u32[]{:S(2)}) async-start(bf16[64,4,176]{2,1,0:T(4,128)(2,1)} %reshape.266), calls=%async_computation.3 | async-start | bytes 262144 | tf_op jit(solution)/shard_map/all_to_all | solution.py:103
  111.1 24.3 %copy-start.11 = (bf16[176,512]{1,0:T(8,128)(2,1)S(1)}, bf16[176,512]{1,0:T(8,128)(2,1)}, u32[]{:S(2)}) copy-start(bf16[176,512]{1,0:T(8,128)(2,1)} %param.14) | copy-start | bytes 540676
  121.5 101.6 %all-to-all-start = ((bf16[2,176,4096]{1,0,2:T(2,128)(2,1)}), bf16[2,176,4096]{1,0,2:T(2,128)(2,1)}, u32[]{:S(2)}, u32[]{:S(2)}) async-start(bf16[2,176,4096]{1,0,2:T(2,128)(2,1)} %copy.41), calls=%async_computation | async-start | bytes 8388608 | tf_op jit(solution)/shard_map/all_to_all | solution.py:203
  127.2 28.3 %copy-start.2 = (bf16[3,176,1408]{2,1,0:T(8,128)(2,1)S(1)}, bf16[3,176,1408]{2,1,0:T(8,128)(2,1)}, u32[]{:S(2)}) copy-start(bf16[3,176,1408]{2,1,0:T(8,128)(2,1)} %param.16) | copy-start | bytes 4460548
  149.0 7.8 %collective-permute-start.1 = (bf16[176,512]{1,0:T(8,128)(2,1)S(1)}, bf16[176,512]{1,0:T(8,128)(2,1)S(1)}, u32[]{:S(2)}, u32[]{:S(2)}) collective-permute-start(bf16[176,512]{1,0:T(8,128)(2,1)S(1)} %multiply_convert_fusion), channel_id=1, source_target_pairs={{0,64},{64,128},{128,192},{192,256},{256,320},{320,384},{384,448},... | collective-permute-start | bytes 540680 | tf_op jit(solution)/shard_map/ppermute | solution.py:137
  151.4 7.4 %collective-permute-start = (bf16[176,512]{1,0:T(8,128)(2,1)S(1)}, bf16[176,512]{1,0:T(8,128)(2,1)S(1)}, u32[]{:S(2)}, u32[]{:S(2)}) collective-permute-start(bf16[176,512]{1,0:T(8,128)(2,1)S(1)} %multiply_convert_fusion), channel_id=1, source_target_pairs={{0,448},{64,0},{128,64},{192,128},{256,192},{320,256},{384,320},{4... | collective-permute-start | bytes 540680 | tf_op jit(solution)/shard_map/ppermute | solution.py:139
  156.8 7.8 %collective-permute-start.3 = (bf16[176,512]{1,0:T(8,128)(2,1)S(1)}, bf16[176,512]{1,0:T(8,128)(2,1)S(1)}, u32[]{:S(2)}, u32[]{:S(2)}) collective-permute-start(bf16[176,512]{1,0:T(8,128)(2,1)S(1)} %collective-permute-done.1), channel_id=1, source_target_pairs={{0,64},{64,128},{128,192},{192,256},{256,320},{320,384},{384,448},... | collective-permute-start | bytes 540680 | tf_op jit(solution)/shard_map/ppermute | solution.py:137
  158.7 7.8 %collective-permute-start.2 = (bf16[176,512]{1,0:T(8,128)(2,1)S(1)}, bf16[176,512]{1,0:T(8,128)(2,1)S(1)}, u32[]{:S(2)}, u32[]{:S(2)}) collective-permute-start(bf16[176,512]{1,0:T(8,128)(2,1)S(1)} %collective-permute-done), channel_id=1, source_target_pairs={{0,448},{64,0},{128,64},{192,128},{256,192},{320,256},{384,320},{4... | collective-permute-start | bytes 540680 | tf_op jit(solution)/shard_map/ppermute | solution.py:139
  164.7 7.8 %collective-permute-start.5 = (bf16[176,512]{1,0:T(8,128)(2,1)S(1)}, bf16[176,512]{1,0:T(8,128)(2,1)S(1)}, u32[]{:S(2)}, u32[]{:S(2)}) collective-permute-start(bf16[176,512]{1,0:T(8,128)(2,1)S(1)} %collective-permute-done.3), channel_id=1, source_target_pairs={{0,64},{64,128},{128,192},{192,256},{256,320},{320,384},{384,448},... | collective-permute-start | bytes 540680 | tf_op jit(solution)/shard_map/ppermute | solution.py:137
  166.6 8.2 %collective-permute-start.4 = (bf16[176,512]{1,0:T(8,128)(2,1)S(1)}, bf16[176,512]{1,0:T(8,128)(2,1)S(1)}, u32[]{:S(2)}, u32[]{:S(2)}) collective-permute-start(bf16[176,512]{1,0:T(8,128)(2,1)S(1)} %collective-permute-done.2), channel_id=1, source_target_pairs={{0,448},{64,0},{128,64},{192,128},{256,192},{320,256},{384,320},{4... | collective-permute-start | bytes 540680 | tf_op jit(solution)/shard_map/ppermute | solution.py:139
  172.5 7.8 %collective-permute-start.6 = (bf16[176,512]{1,0:T(8,128)(2,1)S(1)}, bf16[176,512]{1,0:T(8,128)(2,1)S(1)}, u32[]{:S(2)}, u32[]{:S(2)}) collective-permute-start(bf16[176,512]{1,0:T(8,128)(2,1)S(1)} %collective-permute-done.5), channel_id=1, source_target_pairs={{0,64},{64,128},{128,192},{192,256},{256,320},{320,384},{384,448},... | collective-permute-start | bytes 540680 | tf_op jit(solution)/shard_map/ppermute | solution.py:137
  180.7 1.7 copy-start.6
  181.8 2.6 copy-start.8
  182.4 1.4 copy-start.3
  242.7 9.8 %copy-start.9 = (bf16[2,44,512]{2,1,0:T(8,128)(2,1)S(1)}, bf16[2,44,512]{2,1,0:T(8,128)(2,1)}, u32[]{:S(2)}) copy-start(bf16[2,44,512]{2,1,0:T(8,128)(2,1)} %copy-done.8) | copy-start | bytes 270340
  255.3 4.9 %copy-start.4 = (f32[2,512,512]{1,2,0:T(8,128)S(1)}, f32[2,512,512]{1,2,0:T(8,128)}, u32[]{:S(2)}) copy-start(f32[2,512,512]{1,2,0:T(8,128)} %copy-done.3) | copy-start | bytes 6291460
  255.4 4.9 %copy-start.7 = (bf16[1,176,512]{2,1,0:T(8,128)(2,1)S(1)}, bf16[1,176,512]{2,1,0:T(8,128)(2,1)}, u32[]{:S(2)}) copy-start(bf16[1,176,512]{2,1,0:T(8,128)(2,1)} %copy-done.6) | copy-start | bytes 540676
  261.8 13.2 %copy-start.1 = (bf16[4,176,1408]{2,1,0:T(8,128)(2,1)S(1)}, bf16[4,176,1408]{2,1,0:T(8,128)(2,1)}, u32[]{:S(2)}) copy-start(bf16[4,176,1408]{2,1,0:T(8,128)(2,1)} %param.12) | copy-start | bytes 5947396
Sparse Core Ops, SparseCore 0:
  44.1 36.3 reduce-scatter.3
